TPU v7x, 32 devices: a whole 2x2x4 slice. The times are simulated.
32 devices in a mesh: row: 4 (over x, core), col: 2 (over y), reg: 4 (over z).
Axes of the slice: x: 2, y: 2, z: 4, core: 2. Of those that a mesh axis runs over, the one named last changes fastest.
Arguments:
- activity: bfloat16 [24576, 2048], P(('row', 'col', 'reg')), may hold values from -6 to 6
- basis: bfloat16 [24576, 64], P(('row', 'col', 'reg')), may hold values from -0.21875 to 0.21875
- region_of: int32 [192], P(('row', 'col', 'reg')), may hold values from 0 to 3
- pairs: int32 [1024, 2], P(('row', 'col', 'reg')), may hold values from 0 to 15, as said below
- lags: int32 [8], replicated, may hold values from 0 to 7, each once
Outputs:
- covariance: bfloat16 [1024, 64, 512], P(('row', 'col', 'reg'))
Inputs may be any that keep to these rules, and one draw needn't show every extreme that they name: pairs[p, 0] is below 8 and pairs[p, 1] below 16.
All inputs are finite; a program needn't handle non-finite values.
Results may differ from a plain program's by a relative error of at most 0.0055.
Values may be sent and summed in bfloat16 or wider, within the bound.
A program may use at most 128 MiB of HBM per device.

v0:
```python
import jax
import jax.numpy as jnp
from jax import lax
from jax.sharding import PartitionSpec as P

BLK = 128


def local(activity, basis, region_of, pairs, lags):
    width = basis.shape[1]
    bins = activity.shape[1]
    own = lax.axis_index("reg")
    cell_act, cell_basis, cell_region = (
        lax.all_gather(activity, "reg", axis=0, tiled=True),
        lax.all_gather(basis, "reg", axis=0, tiled=True),
        lax.all_gather(region_of, "reg", axis=0, tiled=True),
    )
    row_region = jnp.repeat(cell_region, BLK)
    masked = jnp.where((row_region == own)[:, None], cell_basis, jnp.zeros((), jnp.bfloat16))
    region_sum = lax.dot_general(
        masked, cell_act, (((0,), (0,)), ((), ())), preferred_element_type=jnp.float32
    )
    panel = region_sum.reshape(1, width, bins).astype(jnp.bfloat16)
    lefts = lax.all_gather(panel, ("col", "reg"), axis=0, tiled=True)
    rights = lax.all_gather(panel, ("row", "reg"), axis=0, tiled=True)
    nlag = lags.shape[0]
    padded = jnp.pad(rights, ((0, 0), (0, 0), (0, nlag)))
    scale = 1.0 / bins**0.5

    def one_pair(pair):
        left_panel = lefts[pair[0]]
        right_panel = padded[pair[1]]
        blocks_out = []
        for m in range(nlag):
            shifted = lax.dynamic_slice_in_dim(right_panel, lags[m], bins, 1)
            blocks_out.append(
                lax.dot_general(
                    left_panel,
                    shifted,
                    (((1,), (1,)), ((), ())),
                    preferred_element_type=jnp.float32,
                )
            )
        prod = jnp.concatenate(blocks_out, axis=1)
        return (prod * scale).astype(jnp.bfloat16)

    return lax.map(one_pair, pairs)


def solution(mesh):
    return jax.shard_map(
        local,
        mesh=mesh,
        in_specs=(
            P(("row", "col", "reg"), None),
            P(("row", "col", "reg"), None),
            P(("row", "col", "reg")),
            P(("row", "col", "reg"), None),
            P(),
        ),
        out_specs=P(("row", "col", "reg"), None, None),
        check_vma=False,
    )
```

profile of v0, /device:TPU:0, one launch (start us, length us, event | category | flops | bytes accessed | tf_op | source)
XLA Modules:
  0.0 840.4 jit_solution(15128685698850178656)
XLA Ops:
  8.8 9.9 %all-reduce.1 = s32[24]{0:T(128)S(1)} all-reduce(s32[24]{0:T(128)S(1)} %dynamic-update-slice), channel_id=1, replica_groups=mesh['row'=4,'col'=2,'reg'=4] {'reg'}, use_global_device_ids=true, to_apply=%add.1 | all-reduce | flops 24 | bytes 192
  18.7 28.5 %all_gather.16 = bf16[3072,64]{0,1:T(8,128)(2,1)S(1)} all-gather(bf16[768,64]{0,1:T(8,128)(2,1)S(1)} %copy-done.1), channel_id=1, replica_groups=mesh['row'=4,'col'=2,'reg'=4] {'reg'}, dimensions={0}, use_global_device_ids=true | all-gather | bytes 491520 | tf_op jit(solution)/shard_map/all_gather | solution.py:15
  47.3 185.3 %all-gather.6.cloned.1.call-done = bf16[3072,2048]{1,0:T(8,128)(2,1)} async-done(((bf16[768,2048]{1,0:T(8,128)(2,1)}), bf16[3072,2048]{1,0:T(8,128)(2,1)}) %all-gather.6.cloned.1.call-update) | async-done | bytes 12582928 | tf_op jit(solution)/shard_map/all_gather | solution.py:14
  232.6 7.6 convolution_convert_fusion
  256.3 33.9 %all-gather.10.cloned.1.call-done = bf16[1024,2048]{1,0:T(8,128)(2,1)} async-done(((bf16[64,2048]{1,0:T(8,128)(2,1)}), bf16[1024,2048]{1,0:T(8,128)(2,1)}) %all-gather.10.cloned.1.call-update) | async-done | bytes 4194320 | tf_op jit(solution)/shard_map/all_gather | solution.py:25
  290.3 4.7 pad.4
  295.0 45.2 %all-gather.8.cloned.1.call-done = bf16[512,2048]{1,0:T(8,128)(2,1)} async-done(((bf16[64,2048]{1,0:T(8,128)(2,1)}), bf16[512,2048]{1,0:T(8,128)(2,1)}) %all-gather.8.cloned.1.call-update) | async-done | bytes 2097168 | tf_op jit(solution)/shard_map/all_gather | solution.py:24
  340.2 493.7 %while.13 = (s32[]{:T(128)}, bf16[32,64,512]{2,1,0:T(8,128)(2,1)}, s32[32,2]{0,1:T(2,128)S(1)}, bf16[8,64,2048]{2,1,0:T(8,128)(2,1)}, bf16[16,64,2056]{2,1,0:T(8...) while((s32[]{:T(128)}, bf16[32,64,512]{2,1,0:T(8,128)(2,1)}, ...), condition=%wide.region_1.2_spmd, body=%wide.region_0.1_spmd.sunk | while | flops 134283264 | bytes 13177721 | solution.py:47
  344.4 1.3 convolution_bitcast_fusion.17
  345.8 1.3 convolution_bitcast_fusion.18
  347.1 1.3 convolution_bitcast_fusion.19
  359.9 1.3 convolution_bitcast_fusion.17
  362.5 1.3 convolution_bitcast_fusion.19
  375.3 1.3 convolution_bitcast_fusion.17
  378.0 1.3 convolution_bitcast_fusion.19
  390.7 1.3 convolution_bitcast_fusion.17
  393.4 1.3 convolution_bitcast_fusion.19
  406.1 1.3 convolution_bitcast_fusion.17
  408.8 1.3 convolution_bitcast_fusion.19
  421.6 1.3 convolution_bitcast_fusion.17
  424.3 1.3 convolution_bitcast_fusion.19
  437.0 1.3 convolution_bitcast_fusion.17
  439.7 1.3 convolution_bitcast_fusion.19
  452.4 1.3 convolution_bitcast_fusion.17
  455.1 1.3 convolution_bitcast_fusion.19
  467.8 1.3 convolution_bitcast_fusion.17
  470.5 1.3 convolution_bitcast_fusion.19
  483.3 1.3 convolution_bitcast_fusion.17
  486.0 1.3 convolution_bitcast_fusion.19
  498.7 1.3 convolution_bitcast_fusion.17
  501.4 1.3 convolution_bitcast_fusion.19
  514.1 1.3 convolution_bitcast_fusion.17
  516.8 1.3 convolution_bitcast_fusion.19
  529.6 1.3 convolution_bitcast_fusion.17
  532.2 1.3 convolution_bitcast_fusion.19
  545.0 1.3 convolution_bitcast_fusion.17
  547.7 1.3 convolution_bitcast_fusion.19
  560.4 1.3 convolution_bitcast_fusion.17
  563.1 1.3 convolution_bitcast_fusion.19
  575.8 1.3 convolution_bitcast_fusion.17
  578.5 1.3 convolution_bitcast_fusion.19
  591.3 1.3 convolution_bitcast_fusion.17
  594.0 1.3 convolution_bitcast_fusion.19
  606.7 1.3 convolution_bitcast_fusion.17
  609.4 1.3 convolution_bitcast_fusion.19
  622.1 1.3 convolution_bitcast_fusion.17
  624.8 1.3 convolution_bitcast_fusion.19
  637.5 1.3 convolution_bitcast_fusion.17
  640.2 1.3 convolution_bitcast_fusion.19
  653.0 1.3 convolution_bitcast_fusion.17
  655.7 1.3 convolution_bitcast_fusion.19
  668.4 1.3 convolution_bitcast_fusion.17
  671.1 1.3 convolution_bitcast_fusion.19
  683.8 1.3 convolution_bitcast_fusion.17
  686.5 1.3 convolution_bitcast_fusion.19
  699.3 1.3 convolution_bitcast_fusion.17
  714.7 1.3 convolution_bitcast_fusion.17
  730.1 1.3 convolution_bitcast_fusion.17
  745.5 1.3 convolution_bitcast_fusion.17
  761.0 1.3 convolution_bitcast_fusion.17
  776.4 1.3 convolution_bitcast_fusion.17
  791.8 1.3 convolution_bitcast_fusion.17
  807.2 1.3 convolution_bitcast_fusion.17
  822.7 1.3 convolution_bitcast_fusion.17
  (415 shorter events, 305.8 us)
Async XLA Ops:
  6.5 0.8 copy-start.5
  6.5 2.0 copy-start.4
  6.5 12.2 %copy-start.1 = (bf16[768,64]{0,1:T(8,128)(2,1)S(1)}, bf16[768,64]{0,1:T(8,128)(2,1)}, u32[]{:S(2)}) copy-start(bf16[768,64]{0,1:T(8,128)(2,1)} %param.8) | copy-start | bytes 294916
  6.5 226.1 %all-gather.6.cloned.1.call-start = ((), (), s32[]{:S(2)}) async-start(), calls=%async_computation | async-start | bytes 15728640 | tf_op jit(solution)/shard_map/all_gather | solution.py:14
  7.3 283.0 %all-gather.10.cloned.1.call-start = ((), (), s32[]{:S(2)}) async-start(), calls=%async_computation.2 | async-start | bytes 4456448 | tf_op jit(solution)/shard_map/all_gather | solution.py:25
  47.3 193.7 %copy-start.2 = (s32[8]{0:T(128)S(1)}, s32[8]{0:T(128)}, u32[]{:S(2)}) copy-start(s32[8]{0:T(128)} %param.11) | copy-start | bytes 100
  240.2 100.0 %all-gather.8.cloned.1.call-start = ((), (), s32[]{:S(2)}) async-start(), calls=%async_computation.1 | async-start | bytes 2359296 | tf_op jit(solution)/shard_map/all_gather | solution.py:24
  290.3 49.9 %copy-start.3 = (s32[32,2]{0,1:T(2,128)S(1)}, s32[32,2]{0,1:T(2,128)}, u32[]{:S(2)}) copy-start(s32[32,2]{0,1:T(2,128)} %param.10) | copy-start | bytes 772
  340.2 9.6 %copy-start = (bf16[8,64,2048]{2,1,0:T(8,128)(2,1)S(1)}, bf16[8,64,2048]{2,1,0:T(8,128)(2,1)}, u32[]{:S(2)}) copy-start(bf16[8,64,2048]{2,1,0:T(8,128)(2,1)} %get-tuple-element.422) | copy-start | bytes 6291460 | tf_op jit(solution)/shard_map/while
  355.6 9.6 %copy-start = (bf16[8,64,2048]{2,1,0:T(8,128)(2,1)S(1)}, bf16[8,64,2048]{2,1,0:T(8,128)(2,1)}, u32[]{:S(2)}) copy-start(bf16[8,64,2048]{2,1,0:T(8,128)(2,1)} %get-tuple-element.422) | copy-start | bytes 6291460 | tf_op jit(solution)/shard_map/while
  371.1 9.6 %copy-start = (bf16[8,64,2048]{2,1,0:T(8,128)(2,1)S(1)}, bf16[8,64,2048]{2,1,0:T(8,128)(2,1)}, u32[]{:S(2)}) copy-start(bf16[8,64,2048]{2,1,0:T(8,128)(2,1)} %get-tuple-element.422) | copy-start | bytes 6291460 | tf_op jit(solution)/shard_map/while
  386.5 9.6 %copy-start = (bf16[8,64,2048]{2,1,0:T(8,128)(2,1)S(1)}, bf16[8,64,2048]{2,1,0:T(8,128)(2,1)}, u32[]{:S(2)}) copy-start(bf16[8,64,2048]{2,1,0:T(8,128)(2,1)} %get-tuple-element.422) | copy-start | bytes 6291460 | tf_op jit(solution)/shard_map/while
  401.9 9.6 %copy-start = (bf16[8,64,2048]{2,1,0:T(8,128)(2,1)S(1)}, bf16[8,64,2048]{2,1,0:T(8,128)(2,1)}, u32[]{:S(2)}) copy-start(bf16[8,64,2048]{2,1,0:T(8,128)(2,1)} %get-tuple-element.422) | copy-start | bytes 6291460 | tf_op jit(solution)/shard_map/while
  417.4 9.6 %copy-start = (bf16[8,64,2048]{2,1,0:T(8,128)(2,1)S(1)}, bf16[8,64,2048]{2,1,0:T(8,128)(2,1)}, u32[]{:S(2)}) copy-start(bf16[8,64,2048]{2,1,0:T(8,128)(2,1)} %get-tuple-element.422) | copy-start | bytes 6291460 | tf_op jit(solution)/shard_map/while
  432.8 9.6 %copy-start = (bf16[8,64,2048]{2,1,0:T(8,128)(2,1)S(1)}, bf16[8,64,2048]{2,1,0:T(8,128)(2,1)}, u32[]{:S(2)}) copy-start(bf16[8,64,2048]{2,1,0:T(8,128)(2,1)} %get-tuple-element.422) | copy-start | bytes 6291460 | tf_op jit(solution)/shard_map/while
  448.2 9.6 %copy-start = (bf16[8,64,2048]{2,1,0:T(8,128)(2,1)S(1)}, bf16[8,64,2048]{2,1,0:T(8,128)(2,1)}, u32[]{:S(2)}) copy-start(bf16[8,64,2048]{2,1,0:T(8,128)(2,1)} %get-tuple-element.422) | copy-start | bytes 6291460 | tf_op jit(solution)/shard_map/while
  463.6 9.6 %copy-start = (bf16[8,64,2048]{2,1,0:T(8,128)(2,1)S(1)}, bf16[8,64,2048]{2,1,0:T(8,128)(2,1)}, u32[]{:S(2)}) copy-start(bf16[8,64,2048]{2,1,0:T(8,128)(2,1)} %get-tuple-element.422) | copy-start | bytes 6291460 | tf_op jit(solution)/shard_map/while
  479.1 9.6 %copy-start = (bf16[8,64,2048]{2,1,0:T(8,128)(2,1)S(1)}, bf16[8,64,2048]{2,1,0:T(8,128)(2,1)}, u32[]{:S(2)}) copy-start(bf16[8,64,2048]{2,1,0:T(8,128)(2,1)} %get-tuple-element.422) | copy-start | bytes 6291460 | tf_op jit(solution)/shard_map/while
  494.5 9.6 %copy-start = (bf16[8,64,2048]{2,1,0:T(8,128)(2,1)S(1)}, bf16[8,64,2048]{2,1,0:T(8,128)(2,1)}, u32[]{:S(2)}) copy-start(bf16[8,64,2048]{2,1,0:T(8,128)(2,1)} %get-tuple-element.422) | copy-start | bytes 6291460 | tf_op jit(solution)/shard_map/while
  509.9 9.6 %copy-start = (bf16[8,64,2048]{2,1,0:T(8,128)(2,1)S(1)}, bf16[8,64,2048]{2,1,0:T(8,128)(2,1)}, u32[]{:S(2)}) copy-start(bf16[8,64,2048]{2,1,0:T(8,128)(2,1)} %get-tuple-element.422) | copy-start | bytes 6291460 | tf_op jit(solution)/shard_map/while
  525.3 9.6 %copy-start = (bf16[8,64,2048]{2,1,0:T(8,128)(2,1)S(1)}, bf16[8,64,2048]{2,1,0:T(8,128)(2,1)}, u32[]{:S(2)}) copy-start(bf16[8,64,2048]{2,1,0:T(8,128)(2,1)} %get-tuple-element.422) | copy-start | bytes 6291460 | tf_op jit(solution)/shard_map/while
  540.8 9.6 %copy-start = (bf16[8,64,2048]{2,1,0:T(8,128)(2,1)S(1)}, bf16[8,64,2048]{2,1,0:T(8,128)(2,1)}, u32[]{:S(2)}) copy-start(bf16[8,64,2048]{2,1,0:T(8,128)(2,1)} %get-tuple-element.422) | copy-start | bytes 6291460 | tf_op jit(solution)/shard_map/while
  556.2 9.6 %copy-start = (bf16[8,64,2048]{2,1,0:T(8,128)(2,1)S(1)}, bf16[8,64,2048]{2,1,0:T(8,128)(2,1)}, u32[]{:S(2)}) copy-start(bf16[8,64,2048]{2,1,0:T(8,128)(2,1)} %get-tuple-element.422) | copy-start | bytes 6291460 | tf_op jit(solution)/shard_map/while
  571.6 9.6 %copy-start = (bf16[8,64,2048]{2,1,0:T(8,128)(2,1)S(1)}, bf16[8,64,2048]{2,1,0:T(8,128)(2,1)}, u32[]{:S(2)}) copy-start(bf16[8,64,2048]{2,1,0:T(8,128)(2,1)} %get-tuple-element.422) | copy-start | bytes 6291460 | tf_op jit(solution)/shard_map/while
  587.1 9.6 %copy-start = (bf16[8,64,2048]{2,1,0:T(8,128)(2,1)S(1)}, bf16[8,64,2048]{2,1,0:T(8,128)(2,1)}, u32[]{:S(2)}) copy-start(bf16[8,64,2048]{2,1,0:T(8,128)(2,1)} %get-tuple-element.422) | copy-start | bytes 6291460 | tf_op jit(solution)/shard_map/while
  602.5 9.6 %copy-start = (bf16[8,64,2048]{2,1,0:T(8,128)(2,1)S(1)}, bf16[8,64,2048]{2,1,0:T(8,128)(2,1)}, u32[]{:S(2)}) copy-start(bf16[8,64,2048]{2,1,0:T(8,128)(2,1)} %get-tuple-element.422) | copy-start | bytes 6291460 | tf_op jit(solution)/shard_map/while
  617.9 9.6 %copy-start = (bf16[8,64,2048]{2,1,0:T(8,128)(2,1)S(1)}, bf16[8,64,2048]{2,1,0:T(8,128)(2,1)}, u32[]{:S(2)}) copy-start(bf16[8,64,2048]{2,1,0:T(8,128)(2,1)} %get-tuple-element.422) | copy-start | bytes 6291460 | tf_op jit(solution)/shard_map/while
  633.3 9.6 %copy-start = (bf16[8,64,2048]{2,1,0:T(8,128)(2,1)S(1)}, bf16[8,64,2048]{2,1,0:T(8,128)(2,1)}, u32[]{:S(2)}) copy-start(bf16[8,64,2048]{2,1,0:T(8,128)(2,1)} %get-tuple-element.422) | copy-start | bytes 6291460 | tf_op jit(solution)/shard_map/while
  648.8 9.6 %copy-start = (bf16[8,64,2048]{2,1,0:T(8,128)(2,1)S(1)}, bf16[8,64,2048]{2,1,0:T(8,128)(2,1)}, u32[]{:S(2)}) copy-start(bf16[8,64,2048]{2,1,0:T(8,128)(2,1)} %get-tuple-element.422) | copy-start | bytes 6291460 | tf_op jit(solution)/shard_map/while
  664.2 9.6 %copy-start = (bf16[8,64,2048]{2,1,0:T(8,128)(2,1)S(1)}, bf16[8,64,2048]{2,1,0:T(8,128)(2,1)}, u32[]{:S(2)}) copy-start(bf16[8,64,2048]{2,1,0:T(8,128)(2,1)} %get-tuple-element.422) | copy-start | bytes 6291460 | tf_op jit(solution)/shard_map/while
  679.6 9.6 %copy-start = (bf16[8,64,2048]{2,1,0:T(8,128)(2,1)S(1)}, bf16[8,64,2048]{2,1,0:T(8,128)(2,1)}, u32[]{:S(2)}) copy-start(bf16[8,64,2048]{2,1,0:T(8,128)(2,1)} %get-tuple-element.422) | copy-start | bytes 6291460 | tf_op jit(solution)/shard_map/while
  695.0 9.6 %copy-start = (bf16[8,64,2048]{2,1,0:T(8,128)(2,1)S(1)}, bf16[8,64,2048]{2,1,0:T(8,128)(2,1)}, u32[]{:S(2)}) copy-start(bf16[8,64,2048]{2,1,0:T(8,128)(2,1)} %get-tuple-element.422) | copy-start | bytes 6291460 | tf_op jit(solution)/shard_map/while
  710.5 9.6 %copy-start = (bf16[8,64,2048]{2,1,0:T(8,128)(2,1)S(1)}, bf16[8,64,2048]{2,1,0:T(8,128)(2,1)}, u32[]{:S(2)}) copy-start(bf16[8,64,2048]{2,1,0:T(8,128)(2,1)} %get-tuple-element.422) | copy-start | bytes 6291460 | tf_op jit(solution)/shard_map/while
  725.9 9.6 %copy-start = (bf16[8,64,2048]{2,1,0:T(8,128)(2,1)S(1)}, bf16[8,64,2048]{2,1,0:T(8,128)(2,1)}, u32[]{:S(2)}) copy-start(bf16[8,64,2048]{2,1,0:T(8,128)(2,1)} %get-tuple-element.422) | copy-start | bytes 6291460 | tf_op jit(solution)/shard_map/while
  741.3 9.6 %copy-start = (bf16[8,64,2048]{2,1,0:T(8,128)(2,1)S(1)}, bf16[8,64,2048]{2,1,0:T(8,128)(2,1)}, u32[]{:S(2)}) copy-start(bf16[8,64,2048]{2,1,0:T(8,128)(2,1)} %get-tuple-element.422) | copy-start | bytes 6291460 | tf_op jit(solution)/shard_map/while
  756.8 9.6 %copy-start = (bf16[8,64,2048]{2,1,0:T(8,128)(2,1)S(1)}, bf16[8,64,2048]{2,1,0:T(8,128)(2,1)}, u32[]{:S(2)}) copy-start(bf16[8,64,2048]{2,1,0:T(8,128)(2,1)} %get-tuple-element.422) | copy-start | bytes 6291460 | tf_op jit(solution)/shard_map/while
  772.2 9.6 %copy-start = (bf16[8,64,2048]{2,1,0:T(8,128)(2,1)S(1)}, bf16[8,64,2048]{2,1,0:T(8,128)(2,1)}, u32[]{:S(2)}) copy-start(bf16[8,64,2048]{2,1,0:T(8,128)(2,1)} %get-tuple-element.422) | copy-start | bytes 6291460 | tf_op jit(solution)/shard_map/while
  787.6 9.6 %copy-start = (bf16[8,64,2048]{2,1,0:T(8,128)(2,1)S(1)}, bf16[8,64,2048]{2,1,0:T(8,128)(2,1)}, u32[]{:S(2)}) copy-start(bf16[8,64,2048]{2,1,0:T(8,128)(2,1)} %get-tuple-element.422) | copy-start | bytes 6291460 | tf_op jit(solution)/shard_map/while
  803.0 9.6 %copy-start = (bf16[8,64,2048]{2,1,0:T(8,128)(2,1)S(1)}, bf16[8,64,2048]{2,1,0:T(8,128)(2,1)}, u32[]{:S(2)}) copy-start(bf16[8,64,2048]{2,1,0:T(8,128)(2,1)} %get-tuple-element.422) | copy-start | bytes 6291460 | tf_op jit(solution)/shard_map/while
  818.5 9.6 %copy-start = (bf16[8,64,2048]{2,1,0:T(8,128)(2,1)S(1)}, bf16[8,64,2048]{2,1,0:T(8,128)(2,1)}, u32[]{:S(2)}) copy-start(bf16[8,64,2048]{2,1,0:T(8,128)(2,1)} %get-tuple-element.422) | copy-start | bytes 6291460 | tf_op jit(solution)/shard_map/while
Sparse Core Ops, SparseCore 0:
  8.9 223.6 all-gather.5
  240.3 49.9 all-gather.9
  292.4 47.7 all-gather.7
where the time goes:
time: 849 us; the launch traced here: 840 us
  matrix products  340 us (40%)
  waiting for transfers between devices  266 us (31%)
  loops' own time  116 us (14%)
  blocking collectives  38.4 us (5%)
  local copies, waits for them, and re-layouts  31 us (4%)
  between operations  28.5 us (3%)
  other arithmetic  20.7 us (2%)
    dot_general x256, matrix products, one_pair(): lax.dot_general(left_panel, shifted, (((1,), (1,)), ((), ())), preferred_...  332 us
    all_gather x1, waiting for transfers between devices, local(): lax.all_gather(activity, 'reg', axis=0, tiled=True)  185 us
    another operation x1, loops' own time, local(): return lax.map(one_pair, pairs)  116 us
    all_gather x1, waiting for transfers between devices, local(): lefts = lax.all_gather(panel, ('col', 'reg'), axis=0, tiled=True)  45.2 us
    all_gather x1, waiting for transfers between devices, local(): rights = lax.all_gather(panel, ('row', 'reg'), axis=0, tiled=True)  33.9 us
    all_gather x1, blocking collectives, local(): lax.all_gather(basis, 'reg', axis=0, tiled=True)  28.5 us
    dynamic_update_slice x32, other arithmetic, local(): return lax.map(one_pair, pairs)  20.7 us
    slice x32, local copies, waits for them, and re-layouts, one_pair(): left_panel = lefts[pair[0]]  18.7 us
  transfers between devices with their start and end apart: 3, of which 3 were waited for; matrix products, arithmetic and copies ran while one was open for 1% of the time, Pallas kernels for 0%

commit v1 on v0

v1 whole, which is shorter than its diff:
```python
import functools

import jax
import jax.numpy as jnp
from jax import lax
from jax.experimental import pallas as pl
from jax.experimental.pallas import tpu as pltpu
from jax.sharding import PartitionSpec as P

BLK = 128


def shift_right(x, s):
    col = lax.broadcasted_iota(jnp.int32, x.shape, 1)
    return jnp.where(col >= s, pltpu.roll(x, s, 1), 0.0)


def shift_left(x, s):
    bins = x.shape[1]
    col = lax.broadcasted_iota(jnp.int32, x.shape, 1)
    return jnp.where(col < bins - s, pltpu.roll(x, bins - s, 1), 0.0)


def pair_kernel(nlag, pairs_ref, lags_ref, left_ref, right_ref, out_ref, prod):
    left, right = left_ref[0], right_ref[0]
    width, bins = left.shape
    leftf, rightf = left.astype(jnp.float32), right.astype(jnp.float32)
    lhs = jnp.concatenate([left, shift_right(leftf, 1).astype(jnp.bfloat16)], axis=0)
    rhs = jnp.concatenate(
        [right] + [shift_left(rightf, s).astype(jnp.bfloat16) for s in range(2, nlag, 2)], axis=0
    )
    acc = lax.dot_general(
        lhs, rhs, (((1,), (1,)), ((), ())), preferred_element_type=jnp.float32
    )
    acc = acc * (1.0 / bins**0.5)
    for lag in range(nlag):
        m1, m2 = lag % 2, lag // 2
        prod[lag] = acc[m1 * width:(m1 + 1) * width, m2 * width:(m2 + 1) * width]
    out_ref[0] = jnp.concatenate(
        [prod[lags_ref[m]] for m in range(nlag)], axis=1
    ).astype(jnp.bfloat16)


def covariances(lefts, rights, pairs, lags):
    npairs = pairs.shape[0]
    nlag = lags.shape[0]
    _, width, bins = lefts.shape
    return pl.pallas_call(
        functools.partial(pair_kernel, nlag),
        grid_spec=pltpu.PrefetchScalarGridSpec(
            num_scalar_prefetch=2,
            grid=(npairs,),
            in_specs=[
                pl.BlockSpec((1, width, bins), lambda p, pairs, lags: (pairs[p, 0], 0, 0)),
                pl.BlockSpec((1, width, bins), lambda p, pairs, lags: (pairs[p, 1], 0, 0)),
            ],
            out_specs=pl.BlockSpec((1, width, nlag * width), lambda p, pairs, lags: (p, 0, 0)),
            scratch_shapes=[pltpu.VMEM((nlag, width, width), jnp.float32)],
        ),
        out_shape=jax.ShapeDtypeStruct((npairs, width, nlag * width), jnp.bfloat16),
        compiler_params=pltpu.CompilerParams(dimension_semantics=("arbitrary",)),
    )(pairs, lags, lefts, rights)


def local(nreg, activity, basis, region_of, pairs, lags):
    width = basis.shape[1]
    bins = activity.shape[1]
    row_region = jnp.repeat(region_of, BLK)
    match = row_region[:, None] == jnp.arange(nreg, dtype=jnp.int32)[None, :]
    masked = jnp.where(match[:, :, None], basis[:, None, :], jnp.zeros((), jnp.bfloat16))
    masked = masked.reshape(basis.shape[0], nreg * width)
    partial = lax.dot_general(
        masked, activity, (((0,), (0,)), ((), ())), preferred_element_type=jnp.float32
    )
    signal = lax.psum_scatter(partial, "reg", scatter_dimension=0, tiled=True)
    panel = signal.reshape(1, width, bins).astype(jnp.bfloat16)
    lefts = lax.all_gather(panel, ("col", "reg"), axis=0, tiled=True)
    rights = lax.all_gather(panel, ("row", "reg"), axis=0, tiled=True)
    return covariances(lefts, rights, pairs, lags)


def solution(mesh):
    return jax.shard_map(
        functools.partial(local, mesh.shape["reg"]),
        mesh=mesh,
        in_specs=(
            P(("row", "col", "reg"), None),
            P(("row", "col", "reg"), None),
            P(("row", "col", "reg")),
            P(("row", "col", "reg"), None),
            P(),
        ),
        out_specs=P(("row", "col", "reg"), None, None),
        check_vma=False,
    )
```

time: 849 us -> 200 us (0.24)
  matrix products: 340 us -> 2.32 us
  waiting for transfers between devices: 266 us -> 147 us
  loops' own time: 116 us -> 0 us
  blocking collectives: 38.4 us -> 0 us
  Pallas kernels: 0 us -> 32.1 us
  local copies, waits for them, and re-layouts: 31 us -> 1.58 us
  other arithmetic: 20.7 us -> 2.78 us
  between operations: 28.5 us -> 13.1 us
    dot_general x257 -> x1, matrix products: 340 us -> 2.32 us  [local(): lax.dot_general(masked, activity, (((0,), (0,)), ((), ())), preferred_ele...]
    all_gather x1 -> x0, waiting for transfers between devices: 185 us -> none  [local(): lax.all_gather(activity, 'reg', axis=0, tiled=True)]
    another operation x1 -> x0, loops' own time: 116 us -> none  [local(): return lax.map(one_pair, pairs)]
    reduce_scatter x0 -> x1, waiting for transfers between devices: none -> 46.7 us  [local(): signal = lax.psum_scatter(partial, 'reg', scatter_dimension=0, tiled=True)]
    pallas_call x0 -> x1, Pallas kernels: none -> 32.1 us  [covariances(): pl.pallas_call(functools.partial(pair_kernel, nlag), grid_spec=pltpu.Pref...]
    all_gather x1 -> x0, blocking collectives: 28.5 us -> none  [local(): lax.all_gather(basis, 'reg', axis=0, tiled=True)]
    dynamic_update_slice x32 -> x0, other arithmetic: 20.7 us -> none  [local(): return lax.map(one_pair, pairs)]
    slice x33 -> x0, local copies, waits for them, and re-layouts: 19.4 us -> none  [the longest x32 18.7 us: one_pair(): left_panel = lefts[pair[0]]]
  transfers between devices with their start and end apart: 3 -> 3, of which waited for: 3 -> 3; matrix products, arithmetic and copies ran while one was open for 1% -> 0% of each run, Pallas kernels for 0% -> 0%
where the time goes in v1:
time: 200 us; the launch traced here: 199 us
  waiting for transfers between devices  147 us (74%)
  Pallas kernels  32.1 us (16%)
  between operations  13.1 us (7%)
  other arithmetic  2.78 us (1%)
  matrix products  2.32 us (1%)
    all_gather x1, waiting for transfers between devices, local(): rights = lax.all_gather(panel, ('row', 'reg'), axis=0, tiled=True)  51.7 us
    all_gather x1, waiting for transfers between devices, local(): lefts = lax.all_gather(panel, ('col', 'reg'), axis=0, tiled=True)  47.8 us
    reduce_scatter x1, waiting for transfers between devices, local(): signal = lax.psum_scatter(partial, 'reg', scatter_dimension=0, tiled=True)  46.7 us
    pallas_call x1, Pallas kernels, covariances(): pl.pallas_call(functools.partial(pair_kernel, nlag), grid_spec=pltpu.Pref...  32.1 us
  transfers between devices with their start and end apart: 3, of which 3 were waited for; matrix products, arithmetic and copies ran while one was open for 0% of the time, Pallas kernels for 0%

profile of v1, /device:TPU:0, one launch (start us, length us, event | category | flops | bytes accessed | tf_op | source)
XLA Modules:
  0.0 198.8 jit_solution(12873408971708802611)
XLA Ops:
  6.5 0.0 copy-start
  6.5 0.0 reduce-scatter.2.cloned.1.call-start
  6.5 0.9 broadcast_bitcast_fusion
  7.4 1.0 broadcast_select_fusion
  8.4 0.0 copy-done
  8.4 0.0 copy-start.1
  8.4 2.3 %fusion = f32[256,2048]{1,0:T(8,128)} fusion(bf16[768,256]{0,1:T(8,128)(2,1)S(1)} %bitcast.9, bf16[768,2048]{1,0:T(8,128)(2,1)S(1)} %copy-done), kind=kOutput, calls=%fused_computation.3 | convolution fusion | flops 805306368 | bytes 5636096 | tf_op jit(solution)/shard_map/dot_general | solution.py:72
  10.8 0.0 reduce-scatter.2.cloned.1.call-update
  10.8 0.0 all-gather.5.cloned.1.call-start
  10.8 46.7 %reduce-scatter.2.cloned.1.call-done = f32[64,2048]{1,0:T(8,128)} async-done(((f32[256,2048]{1,0:T(8,128)}), f32[64,2048]{1,0:T(8,128)}) %reduce-scatter.2.cloned.1.call-update) | async-done | bytes 524304 | tf_op jit(solution)/shard_map/reduce_scatter | solution.py:75
  57.5 1.8 convert_element_type.6
  59.3 0.0 all-gather.5.cloned.1.call-update
  59.3 0.0 all-gather.7.cloned.1.call-start
  59.4 0.7 all-gather.7.cloned.1.call-update
  60.0 0.0 copy-done.1
  60.1 0.7 copy.8.pairs_ref
  60.7 47.8 %all-gather.5.cloned.1.call-done = bf16[512,2048]{1,0:T(8,128)(2,1)} async-done(((bf16[64,2048]{1,0:T(8,128)(2,1)}), bf16[512,2048]{1,0:T(8,128)(2,1)}) %all-gather.5.cloned.1.call-update) | async-done | bytes 2097168 | tf_op jit(solution)/shard_map/all_gather | solution.py:77
  108.5 51.7 %all-gather.7.cloned.1.call-done = bf16[1024,2048]{1,0:T(8,128)(2,1)} async-done(((bf16[64,2048]{1,0:T(8,128)(2,1)}), bf16[1024,2048]{1,0:T(8,128)(2,1)}) %all-gather.7.cloned.1.call-update) | async-done | bytes 4194320 | tf_op jit(solution)/shard_map/all_gather | solution.py:78
  160.2 32.1 %shard_map.55 = bf16[32,64,512]{2,1,0:T(8,128)(2,1)} custom-call(s32[32,2]{1,0:T(8,128)} %copy.8.pairs_ref, s32[8]{0:T(128)} %lags_ref.1, bf16[8,64,2048]{2,1,0:T(8,128)(2,1)} %bitcast.8, bf16[16,64,2048]{2,1,0:T(8,128)(2,1)} %bitcast.7), custom_call_target="tpu_custom_call" | custom-call | tf_op jit(solution)/shard_map/pallas_call | solution.py:48
  (1 shorter events, 0.0 us)
Async XLA Ops:
  6.5 1.9 copy-start
  6.5 51.0 %reduce-scatter.2.cloned.1.call-start = ((), (), s32[]{:S(2)}) async-start(), calls=%async_computation.1 | async-start | bytes 2621440 | tf_op jit(solution)/shard_map/reduce_scatter | solution.py:75
  8.4 51.6 %copy-start.1 = (s32[32,2]{0,1:T(2,128)S(1)}, s32[32,2]{0,1:T(2,128)}, u32[]{:S(2)}) copy-start(s32[32,2]{0,1:T(2,128)} %param.8) | copy-start | bytes 772
  10.8 97.7 %all-gather.5.cloned.1.call-start = ((), (), s32[]{:S(2)}) async-start(), calls=%async_computation.2 | async-start | bytes 2359296 | tf_op jit(solution)/shard_map/all_gather | solution.py:77
  59.3 100.9 %all-gather.7.cloned.1.call-start = ((), (), s32[]{:S(2)}) async-start(), calls=%async_computation.3 | async-start | bytes 4456448 | tf_op jit(solution)/shard_map/all_gather | solution.py:78
Sparse Core Ops, SparseCore 0:
  10.9 46.5 reduce-scatter.1
  59.9 48.5 all-gather.4
  111.0 49.1 all-gather.6

commit v2 on v1

--- a/solution.py
+++ b/solution.py
@@ -8,6 +8,7 @@
 from jax.sharding import PartitionSpec as P
 
 BLK = 128
+CHUNKS = 2
 
 
 def shift_right(x, s):
@@ -62,26 +63,194 @@
     )(pairs, lags, lefts, rights)
 
 
-def local(nreg, activity, basis, region_of, pairs, lags):
-    width = basis.shape[1]
-    bins = activity.shape[1]
-    row_region = jnp.repeat(region_of, BLK)
-    match = row_region[:, None] == jnp.arange(nreg, dtype=jnp.int32)[None, :]
-    masked = jnp.where(match[:, :, None], basis[:, None, :], jnp.zeros((), jnp.bfloat16))
-    masked = masked.reshape(basis.shape[0], nreg * width)
-    partial = lax.dot_general(
-        masked, activity, (((0,), (0,)), ((), ())), preferred_element_type=jnp.float32
-    )
-    signal = lax.psum_scatter(partial, "reg", scatter_dimension=0, tiled=True)
-    panel = signal.reshape(1, width, bins).astype(jnp.bfloat16)
-    lefts = lax.all_gather(panel, ("col", "reg"), axis=0, tiled=True)
-    rights = lax.all_gather(panel, ("row", "reg"), axis=0, tiled=True)
+def panels_kernel(
+    shape, chunks, region_ref, basis_ref, act_ref, lefts_ref, rights_ref,
+    own, send, landed, stage,
+    rs_send, rs_recv, reg_send, reg_recv, col_send, col_recv,
+    x_send, x_recv, sib_send, sib_recv, fwd_send, fwd_recv, left_sem, right_sem,
+):
+    nrow, ncol, nreg = shape
+    nx = nrow // 2
+    width = basis_ref.shape[1]
+    bins = act_ref.shape[1]
+    span = bins // chunks
+    i, j, g = lax.axis_index("row"), lax.axis_index("col"), lax.axis_index("reg")
+    x, core = i // 2, i % 2
+    sib = x * 2 + 1 - core
+
+    def reg_at(k):
+        return {"reg": (g + k) % nreg}
+
+    def col_at(k):
+        return {"col": (j + k) % ncol}
+
+    def x_at(k):
+        return {"row": ((x + k) % nx) * 2 + core}
+
+    peers = [reg_at(k) for k in range(1, nreg)]
+    peers += [col_at(k) for k in range(1, ncol)]
+    peers += [x_at(k) for k in range(1, nx)]
+    peers += [{"row": sib}]
+    barrier = pltpu.get_barrier_semaphore()
+    for peer in peers:
+        pl.semaphore_signal(
+            barrier, inc=1, device_id=peer, device_id_type=pl.DeviceIdType.MESH
+        )
+
+    def remote(src, dst, send_sem, recv_sem, peer):
+        return pltpu.make_async_remote_copy(
+            src_ref=src, dst_ref=dst, send_sem=send_sem, recv_sem=recv_sem,
+            device_id=peer, device_id_type=pl.DeviceIdType.MESH,
+        )
+
+    sent = []
+
+    def start(*args):
+        copy = remote(*args)
+        copy.start()
+        sent.append(copy)
+
+    def right(row, region, c):
+        return rights_ref.at[row * nreg + region, :, pl.ds(c * span, span)]
+
+    def left(col, region, c):
+        return lefts_ref.at[col * nreg + region, :, pl.ds(c * span, span)]
+
+    pieces = []
+    for n in range(basis_ref.shape[0] // BLK):
+        block = basis_ref[n * BLK:(n + 1) * BLK, :]
+        pieces.append(jnp.concatenate(
+            [jnp.where(region_ref[n] == r, block, jnp.zeros_like(block)) for r in range(nreg)],
+            axis=1,
+        ))
+    masked = jnp.concatenate(pieces, axis=0)
+
+    for c in range(chunks):
+        part = lax.dot_general(
+            masked, act_ref[:, c * span:(c + 1) * span], (((0,), (0,)), ((), ())),
+            preferred_element_type=jnp.float32,
+        )
+        own[c] = part
+        send[c] = part.astype(jnp.bfloat16)
+        if c == 0:
+            pl.semaphore_wait(barrier, len(peers))
+        for k in range(1, nreg):
+            rows = pl.ds(pl.multiple_of((g + k) % nreg * width, width), width)
+            start(
+                send.at[c, rows, :], landed.at[k - 1, c],
+                rs_send.at[k - 1, c], rs_recv.at[k - 1, c], reg_at(k),
+            )
+
+    def spread(src, region, q, c):
+        for k in range(1, nx):
+            start(src, right(i, region, c), x_send.at[k - 1, q, c], x_recv.at[k - 1, q, c], x_at(k))
+        for k in range(1, ncol):
+            start(src, left(j, region, c), col_send.at[k - 1, q, c], col_recv.at[k - 1, q, c], col_at(k))
+        start(src, right(i, region, c), sib_send.at[q, c], sib_recv.at[q, c], {"row": sib})
+        copy = pltpu.make_async_copy(src, left(j, region, c), left_sem.at[q, c])
+        copy.start()
+        return copy
+
+    kept = []
+    for c in range(chunks):
+        total = own[c, pl.ds(pl.multiple_of(g * width, width), width), :]
+        for k in range(1, nreg):
+            remote(
+                landed.at[k - 1, c], landed.at[k - 1, c],
+                rs_send.at[k - 1, c], rs_recv.at[k - 1, c], reg_at(k),
+            ).wait_recv()
+            total = total + landed[k - 1, c].astype(jnp.float32)
+        stage[c] = total.astype(jnp.bfloat16)
+        for k in range(1, nreg):
+            start(
+                stage.at[c], right(i, g, c),
+                reg_send.at[k - 1, c], reg_recv.at[k - 1, c], reg_at(k),
+            )
+        copy = pltpu.make_async_copy(stage.at[c], right(i, g, c), right_sem.at[c])
+        copy.start()
+        kept += [copy, spread(stage.at[c], g, 0, c)]
+
+    def region_at(q):
+        return (g - q + nreg) % nreg
+
+    for c in range(chunks):
+        for q in range(1, nreg):
+            here = right(i, region_at(q), c)
+            remote(here, here, reg_send.at[q - 1, c], reg_recv.at[q - 1, c], reg_at(q)).wait_recv()
+            kept.append(spread(here, region_at(q), q, c))
+
+    for c in range(chunks):
+        for q in range(nreg):
+            for k in range(1, nx):
+                here = right((x - k + nx) % nx * 2 + core, region_at(q), c)
+                remote(here, here, x_send.at[k - 1, q, c], x_recv.at[k - 1, q, c], x_at(k)).wait_recv()
+                start(
+                    here, here, fwd_send.at[k - 1, q, c], fwd_recv.at[k - 1, q, c], {"row": sib}
+                )
+
+    for c in range(chunks):
+        for q in range(nreg):
+            region = region_at(q)
+            for k in range(1, ncol):
+                here = left((j - k + ncol) % ncol, region, c)
+                remote(here, here, col_send.at[k - 1, q, c], col_recv.at[k - 1, q, c], col_at(k)).wait_recv()
+            here = right(sib, region, c)
+            remote(here, here, sib_send.at[q, c], sib_recv.at[q, c], {"row": sib}).wait_recv()
+            for k in range(1, nx):
+                here = right((x - k + nx) % nx * 2 + 1 - core, region, c)
+                remote(here, here, fwd_send.at[k - 1, q, c], fwd_recv.at[k - 1, q, c], {"row": sib}).wait_recv()
+    for copy in sent:
+        copy.wait_send()
+    for copy in kept:
+        copy.wait()
+
+
+def gathered_panels(shape, activity, basis, region_of):
+    nrow, ncol, nreg = shape
+    nx = nrow // 2
+    width, bins = basis.shape[1], activity.shape[1]
+    chunks = CHUNKS
+    span = bins // chunks
+    dma = pltpu.SemaphoreType.DMA
+    return pl.pallas_call(
+        functools.partial(panels_kernel, shape, chunks),
+        in_specs=[
+            pl.BlockSpec(memory_space=pltpu.SMEM),
+            pl.BlockSpec(memory_space=pltpu.VMEM),
+            pl.BlockSpec(memory_space=pltpu.VMEM),
+        ],
+        out_specs=[pl.BlockSpec(memory_space=pl.ANY)] * 2,
+        out_shape=[
+            jax.ShapeDtypeStruct((ncol * nreg, width, bins), jnp.bfloat16),
+            jax.ShapeDtypeStruct((nrow * nreg, width, bins), jnp.bfloat16),
+        ],
+        scratch_shapes=[
+            pltpu.VMEM((chunks, nreg * width, span), jnp.float32),
+            pltpu.VMEM((chunks, nreg * width, span), jnp.bfloat16),
+            pltpu.VMEM((nreg - 1, chunks, width, span), jnp.bfloat16),
+            pltpu.VMEM((chunks, width, span), jnp.bfloat16),
+        ]
+        + [dma((nreg - 1, chunks))] * 4
+        + [dma((ncol - 1, nreg, chunks))] * 2
+        + [dma((nx - 1, nreg, chunks))] * 2
+        + [dma((nreg, chunks))] * 2
+        + [dma((nx - 1, nreg, chunks))] * 2
+        + [dma((nreg, chunks)), dma((chunks,))],
+        compiler_params=pltpu.CompilerParams(
+            collective_id=0, has_side_effects=True, vmem_limit_bytes=40 << 20
+        ),
+    )(region_of, basis, activity)
+
+
+def local(shape, activity, basis, region_of, pairs, lags):
+    lefts, rights = gathered_panels(shape, activity, basis, region_of)
     return covariances(lefts, rights, pairs, lags)
 
 
 def solution(mesh):
+    shape = (mesh.shape["row"], mesh.shape["col"], mesh.shape["reg"])
     return jax.shard_map(
-        functools.partial(local, mesh.shape["reg"]),
+        functools.partial(local, shape),
         mesh=mesh,
         in_specs=(
             P(("row", "col", "reg"), None),

time: 200 us -> 103 us (0.52)
  the two profiles are of different devices: /device:TPU:0 before, /device:TPU:17 now
where the time goes in v2:
time: 103 us; the launch traced here: 102 us
  Pallas kernels  93.3 us (91%)
  local copies, waits for them, and re-layouts  8.21 us (8%)
    pallas_call x1, Pallas kernels, gathered_panels(): pl.pallas_call(functools.partial(panels_kernel, shape, chunks), in_specs=...  61.2 us
    pallas_call x1, Pallas kernels, covariances(): pl.pallas_call(functools.partial(pair_kernel, nlag), grid_spec=pltpu.Pref...  32.1 us
    unnamed x10, local copies, waits for them, and re-layouts  8.21 us

profile of v2, /device:TPU:17, one launch (start us, length us, event | category | flops | bytes accessed | tf_op | source)
XLA Modules:
  0.0 101.5 jit_solution(9940682031722209814)
XLA Ops:
  0.0 1.4 %copy.7.pairs_ref = s32[32,2]{1,0:T(8,128)} copy(s32[32,2]{0,1:T(2,128)} %param.8) | data formatting | bytes 512 | tf_op args[3]
  1.4 1.1 %copy.6.basis_ref = bf16[768,64]{1,0:T(8,128)(2,1)S(1)} copy(bf16[768,64]{0,1:T(8,128)(2,1)} %param.6) | data formatting | bytes 196608 | tf_op args[1]
  2.4 0.0 copy-start.1
  2.4 1.9 %copy-done.1 = bf16[768,2048]{1,0:T(8,128)(2,1)S(1)} copy-done((bf16[768,2048]{1,0:T(8,128)(2,1)S(1)}, bf16[768,2048]{1,0:T(8,128)(2,1)}, u32[]{:S(2)}) %copy-start.1) | copy-done | bytes 3145752
  4.3 0.0 copy-start.3
  4.3 0.7 copy-done.3
  5.0 61.2 %shard_map.55 = (bf16[8,64,2048]{2,1,0:T(8,128)(2,1)S(1)}, bf16[16,64,2048]{2,1,0:T(8,128)(2,1)S(1)}) custom-call(s32[6]{0:T(128)S(1)} %copy-done.3, bf16[768,64]{1,0:T(8,128)(2,1)S(1)} %copy.6.basis_ref, bf16[768,2048]{1,0:T(8,128)(2,1)S(1)} %copy-done.1), custom_call_target="tpu_custom_call" | custom-call | tf_op jit(solution)/shard_map/pallas_call | solution.py:215
  66.1 0.0 copy-start
  66.2 1.9 %copy-done = bf16[16,64,2048]{2,1,0:T(8,128)(2,1)} copy-done((bf16[16,64,2048]{2,1,0:T(8,128)(2,1)}, bf16[16,64,2048]{2,1,0:T(8,128)(2,1)S(1)}, u32[]{:S(2)}) %copy-start) | copy-done | bytes 4194328
  68.1 0.0 copy-start.2
  68.1 1.3 %copy-done.2 = bf16[8,64,2048]{2,1,0:T(8,128)(2,1)} copy-done((bf16[8,64,2048]{2,1,0:T(8,128)(2,1)}, bf16[8,64,2048]{2,1,0:T(8,128)(2,1)S(1)}, u32[]{:S(2)}) %copy-start.2) | copy-done | bytes 2097176
  69.4 32.1 %shard_map.56 = bf16[32,64,512]{2,1,0:T(8,128)(2,1)} custom-call(s32[32,2]{1,0:T(8,128)} %copy.7.pairs_ref, s32[8]{0:T(128)} %lags_ref.1, bf16[8,64,2048]{2,1,0:T(8,128)(2,1)} %copy-done.2, bf16[16,64,2048]{2,1,0:T(8,128)(2,1)} %copy-done), custom_call_target="tpu_custom_call" | custom-call | tf_op jit(solution)/shard_map/pallas_call | solution.py:49
Async XLA Ops:
  2.4 1.9 %copy-start.1 = (bf16[768,2048]{1,0:T(8,128)(2,1)S(1)}, bf16[768,2048]{1,0:T(8,128)(2,1)}, u32[]{:S(2)}) copy-start(bf16[768,2048]{1,0:T(8,128)(2,1)} %act_ref.1) | copy-start | bytes 9437188
  4.3 0.7 copy-start.3
  66.1 1.9 %copy-start = (bf16[16,64,2048]{2,1,0:T(8,128)(2,1)}, bf16[16,64,2048]{2,1,0:T(8,128)(2,1)S(1)}, u32[]{:S(2)}) copy-start(bf16[16,64,2048]{2,1,0:T(8,128)(2,1)S(1)} %get-tuple-element.8.right_ref) | copy-start | bytes 12582916
  68.1 1.3 %copy-start.2 = (bf16[8,64,2048]{2,1,0:T(8,128)(2,1)}, bf16[8,64,2048]{2,1,0:T(8,128)(2,1)S(1)}, u32[]{:S(2)}) copy-start(bf16[8,64,2048]{2,1,0:T(8,128)(2,1)S(1)} %get-tuple-element.7.left_ref) | copy-start | bytes 6291460

commit v3 on v2

--- a/solution.py
+++ b/solution.py
@@ -11,25 +11,28 @@
 CHUNKS = 2
 
 
-def shift_right(x, s):
-    col = lax.broadcasted_iota(jnp.int32, x.shape, 1)
-    return jnp.where(col >= s, pltpu.roll(x, s, 1), 0.0)
-
-
-def shift_left(x, s):
+def shifted(x, s):
     bins = x.shape[1]
-    col = lax.broadcasted_iota(jnp.int32, x.shape, 1)
-    return jnp.where(col < bins - s, pltpu.roll(x, bins - s, 1), 0.0)
-
-
-def pair_kernel(nlag, pairs_ref, lags_ref, left_ref, right_ref, out_ref, prod):
-    left, right = left_ref[0], right_ref[0]
-    width, bins = left.shape
-    leftf, rightf = left.astype(jnp.float32), right.astype(jnp.float32)
-    lhs = jnp.concatenate([left, shift_right(leftf, 1).astype(jnp.bfloat16)], axis=0)
-    rhs = jnp.concatenate(
-        [right] + [shift_left(rightf, s).astype(jnp.bfloat16) for s in range(2, nlag, 2)], axis=0
-    )
+    moved = pltpu.roll(x, (bins - s) % bins, 1)
+    edge = moved[:, bins - BLK:] if s > 0 else moved[:, :BLK]
+    col = lax.broadcasted_iota(jnp.int32, edge.shape, 1)
+    if s > 0:
+        edge = jnp.where(col < BLK - s, edge, jnp.zeros_like(edge))
+        return jnp.concatenate([moved[:, :bins - BLK], edge], axis=1)
+    edge = jnp.where(col >= -s, edge, jnp.zeros_like(edge))
+    return jnp.concatenate([edge, moved[:, BLK:]], axis=1)
+
+
+def left_stack(left):
+    return [left, shifted(left, -1)]
+
+
+def right_stack(right, nlag):
+    return [right] + [shifted(right, s) for s in range(2, nlag, 2)]
+
+
+def one_pair(nlag, lags_ref, lhs, rhs, prod):
+    width, bins = lhs.shape[0] // 2, lhs.shape[1]
     acc = lax.dot_general(
         lhs, rhs, (((1,), (1,)), ((), ())), preferred_element_type=jnp.float32
     )
@@ -37,17 +40,69 @@
     for lag in range(nlag):
         m1, m2 = lag % 2, lag // 2
         prod[lag] = acc[m1 * width:(m1 + 1) * width, m2 * width:(m2 + 1) * width]
-    out_ref[0] = jnp.concatenate(
-        [prod[lags_ref[m]] for m in range(nlag)], axis=1
-    ).astype(jnp.bfloat16)
+    return jnp.concatenate([prod[lags_ref[m]] for m in range(nlag)], axis=1).astype(jnp.bfloat16)
+
+
+def pair_kernel(nlag, group, pairs_ref, lags_ref, lefts_ref, rights_ref, out_ref, lhs, rhs, prod):
+    width = lefts_ref.shape[1]
+    step = pl.program_id(0)
+
+    @pl.when(step == 0)
+    def _():
+        @pl.loop(0, lefts_ref.shape[0])
+        def _(r):
+            for m, x in enumerate(left_stack(lefts_ref[r])):
+                lhs[r, m * width:(m + 1) * width, :] = x
+
+        @pl.loop(0, rights_ref.shape[0])
+        def _(r):
+            for m, x in enumerate(right_stack(rights_ref[r], nlag)):
+                rhs[r, m * width:(m + 1) * width, :] = x
+
+    for q in range(group):
+        p = step * group + q
+        out_ref[q] = one_pair(
+            nlag, lags_ref, lhs[pairs_ref[p, 0]], rhs[pairs_ref[p, 1]], prod.at[q]
+        )
+
+
+def stream_kernel(nlag, pairs_ref, lags_ref, left_ref, right_ref, out_ref, prod):
+    lhs = jnp.concatenate(left_stack(left_ref[0]), axis=0)
+    rhs = jnp.concatenate(right_stack(right_ref[0], nlag), axis=0)
+    out_ref[0] = one_pair(nlag, lags_ref, lhs, rhs, prod)
 
 
 def covariances(lefts, rights, pairs, lags):
     npairs = pairs.shape[0]
     nlag = lags.shape[0]
     _, width, bins = lefts.shape
+    out_shape = jax.ShapeDtypeStruct((npairs, width, nlag * width), jnp.bfloat16)
+    panels = 3 * lefts.shape[0] + 5 * rights.shape[0]
+    params = pltpu.CompilerParams(
+        dimension_semantics=("arbitrary",), vmem_limit_bytes=48 << 20
+    )
+    if panels * width * bins * 2 <= 36 << 20:
+        group = 4
+        return pl.pallas_call(
+            functools.partial(pair_kernel, nlag, group),
+            grid_spec=pltpu.PrefetchScalarGridSpec(
+                num_scalar_prefetch=2,
+                grid=(npairs // group,),
+                in_specs=[pl.BlockSpec(memory_space=pltpu.VMEM)] * 2,
+                out_specs=pl.BlockSpec(
+                    (group, width, nlag * width), lambda p, pairs, lags: (p, 0, 0)
+                ),
+                scratch_shapes=[
+                    pltpu.VMEM((lefts.shape[0], 2 * width, bins), jnp.bfloat16),
+                    pltpu.VMEM((rights.shape[0], nlag // 2 * width, bins), jnp.bfloat16),
+                    pltpu.VMEM((group, nlag, width, width), jnp.float32),
+                ],
+            ),
+            out_shape=out_shape,
+            compiler_params=params,
+        )(pairs, lags, lefts, rights)
     return pl.pallas_call(
-        functools.partial(pair_kernel, nlag),
+        functools.partial(stream_kernel, nlag),
         grid_spec=pltpu.PrefetchScalarGridSpec(
             num_scalar_prefetch=2,
             grid=(npairs,),
@@ -58,8 +113,8 @@
             out_specs=pl.BlockSpec((1, width, nlag * width), lambda p, pairs, lags: (p, 0, 0)),
             scratch_shapes=[pltpu.VMEM((nlag, width, width), jnp.float32)],
         ),
-        out_shape=jax.ShapeDtypeStruct((npairs, width, nlag * width), jnp.bfloat16),
-        compiler_params=pltpu.CompilerParams(dimension_semantics=("arbitrary",)),
+        out_shape=out_shape,
+        compiler_params=params,
     )(pairs, lags, lefts, rights)
 
 

time: 103 us -> 91.4 us (0.89)
  the two profiles are of different devices: /device:TPU:17 before, /device:TPU:25 now
where the time goes in v3:
time: 91.4 us; the launch traced here: 91.2 us
  Pallas kernels  84.9 us (93%)
  local copies, waits for them, and re-layouts  6.3 us (7%)
    pallas_call x1, Pallas kernels, gathered_panels(): pl.pallas_call(functools.partial(panels_kernel, shape, chunks), in_specs=...  61.2 us
    pallas_call x1, Pallas kernels, covariances(): pl.pallas_call(functools.partial(pair_kernel, nlag, group), grid_spec=plt...  23.7 us
    unnamed x10, local copies, waits for them, and re-layouts  6.3 us

profile of v3, /device:TPU:25, one launch (start us, length us, event | category | flops | bytes accessed | tf_op | source)
XLA Modules:
  0.0 91.2 jit_solution(14751719790593370410)
XLA Ops:
  0.0 0.0 copy-start.2
  0.0 0.8 copy.7.pairs_ref
  0.8 1.1 %copy.6.basis_ref = bf16[768,64]{1,0:T(8,128)(2,1)S(1)} copy(bf16[768,64]{0,1:T(8,128)(2,1)} %param.6) | data formatting | bytes 196608 | tf_op args[1]
  1.8 0.0 copy-start.1
  1.8 1.9 %copy-done.1 = bf16[768,2048]{1,0:T(8,128)(2,1)S(1)} copy-done((bf16[768,2048]{1,0:T(8,128)(2,1)S(1)}, bf16[768,2048]{1,0:T(8,128)(2,1)}, u32[]{:S(2)}) %copy-start.1) | copy-done | bytes 3145752
  3.7 0.0 copy-start.3
  3.7 0.7 copy-done.3
  4.4 61.2 %shard_map.55 = (bf16[8,64,2048]{2,1,0:T(8,128)(2,1)S(1)}, bf16[16,64,2048]{2,1,0:T(8,128)(2,1)S(1)}) custom-call(s32[6]{0:T(128)S(1)} %copy-done.3, bf16[768,64]{1,0:T(8,128)(2,1)S(1)} %copy.6.basis_ref, bf16[768,2048]{1,0:T(8,128)(2,1)S(1)} %copy-done.1), custom_call_target="tpu_custom_call" | custom-call | tf_op jit(solution)/shard_map/pallas_call | solution.py:270
  65.6 0.0 copy-start
  65.6 1.9 %copy-done = bf16[16,64,2048]{2,1,0:T(8,128)(2,1)} copy-done((bf16[16,64,2048]{2,1,0:T(8,128)(2,1)}, bf16[16,64,2048]{2,1,0:T(8,128)(2,1)S(1)}, u32[]{:S(2)}) %copy-start) | copy-done | bytes 4194328
  67.5 0.0 copy-done.2
  67.5 23.7 %shard_map.56 = bf16[32,64,512]{2,1,0:T(8,128)(2,1)} custom-call(s32[32,2]{1,0:T(8,128)S(1)} %copy.7.pairs_ref, s32[8]{0:T(128)S(1)} %copy-done.2, bf16[8,64,2048]{2,1,0:T(8,128)(2,1)S(1)} %get-tuple-element.7.lefts_ref, bf16[16,64,2048]{2,1,0:T(8,128)(2,1)} %copy-done), custom_call_target="tpu_custom_call" | custom-call | tf_op jit(solution)/shard_map/pallas_call | solution.py:86
Async XLA Ops:
  0.0 67.5 %copy-start.2 = (s32[8]{0:T(128)S(1)}, s32[8]{0:T(128)}, u32[]{:S(2)}) copy-start(s32[8]{0:T(128)} %lags_ref.1) | copy-start | bytes 100
  1.8 1.9 %copy-start.1 = (bf16[768,2048]{1,0:T(8,128)(2,1)S(1)}, bf16[768,2048]{1,0:T(8,128)(2,1)}, u32[]{:S(2)}) copy-start(bf16[768,2048]{1,0:T(8,128)(2,1)} %act_ref.1) | copy-start | bytes 9437188
  3.7 0.7 copy-start.3
  65.6 1.9 %copy-start = (bf16[16,64,2048]{2,1,0:T(8,128)(2,1)}, bf16[16,64,2048]{2,1,0:T(8,128)(2,1)S(1)}, u32[]{:S(2)}) copy-start(bf16[16,64,2048]{2,1,0:T(8,128)(2,1)S(1)} %get-tuple-element.8.rights_ref) | copy-start | bytes 12582916

commit v4 on v3

--- a/solution.py
+++ b/solution.py
@@ -8,7 +8,7 @@
 from jax.sharding import PartitionSpec as P
 
 BLK = 128
-CHUNKS = 2
+CHUNKS = 4
 
 
 def shifted(x, s):
@@ -180,7 +180,7 @@
         ))
     masked = jnp.concatenate(pieces, axis=0)
 
-    for c in range(chunks):
+    def send_partials(c):
         part = lax.dot_general(
             masked, act_ref[:, c * span:(c + 1) * span], (((0,), (0,)), ((), ())),
             preferred_element_type=jnp.float32,
@@ -196,18 +196,32 @@
                 rs_send.at[k - 1, c], rs_recv.at[k - 1, c], reg_at(k),
             )
 
-    def spread(src, region, q, c):
+    def spread(src, s, c):
         for k in range(1, nx):
-            start(src, right(i, region, c), x_send.at[k - 1, q, c], x_recv.at[k - 1, q, c], x_at(k))
+            remote(src, right(i, s, c), x_send.at[k - 1, s, c], x_recv.at[k - 1, s, c], x_at(k)).start()
         for k in range(1, ncol):
-            start(src, left(j, region, c), col_send.at[k - 1, q, c], col_recv.at[k - 1, q, c], col_at(k))
-        start(src, right(i, region, c), sib_send.at[q, c], sib_recv.at[q, c], {"row": sib})
-        copy = pltpu.make_async_copy(src, left(j, region, c), left_sem.at[q, c])
-        copy.start()
-        return copy
-
-    kept = []
-    for c in range(chunks):
+            remote(src, left(j, s, c), col_send.at[k - 1, s, c], col_recv.at[k - 1, s, c], col_at(k)).start()
+        remote(src, right(i, s, c), sib_send.at[s, c], sib_recv.at[s, c], {"row": sib}).start()
+        pltpu.make_async_copy(src, left(j, s, c), left_sem.at[s, c]).start()
+
+    def hop(src, s, d, c, way):
+        to = g + 1 if way == 0 else g - 1
+        return remote(
+            src, right(i, s, c), reg_send.at[way, d, c], reg_recv.at[way, d, c], {"reg": to}
+        )
+
+    def onward(way, d):
+        behind = g - d >= 0 if way == 0 else g + d < nreg
+        ahead = g + 1 < nreg if way == 0 else g >= 1
+        return jnp.logical_and(behind, ahead)
+
+    def origin(way, d):
+        return g - d if way == 0 else g + d
+
+    def has(way, d):
+        return g - d >= 0 if way == 0 else g + d < nreg
+
+    def finish(c):
         total = own[c, pl.ds(pl.multiple_of(g * width, width), width), :]
         for k in range(1, nreg):
             remote(
@@ -216,48 +230,84 @@
             ).wait_recv()
             total = total + landed[k - 1, c].astype(jnp.float32)
         stage[c] = total.astype(jnp.bfloat16)
-        for k in range(1, nreg):
-            start(
-                stage.at[c], right(i, g, c),
-                reg_send.at[k - 1, c], reg_recv.at[k - 1, c], reg_at(k),
-            )
-        copy = pltpu.make_async_copy(stage.at[c], right(i, g, c), right_sem.at[c])
-        copy.start()
-        kept += [copy, spread(stage.at[c], g, 0, c)]
-
-    def region_at(q):
-        return (g - q + nreg) % nreg
+        for way in range(2):
+            @pl.when(onward(way, 0))
+            def _():
+                hop(stage.at[c], g, 0, c, way).start()
+        spread(stage.at[c], g, c)
+        pltpu.make_async_copy(stage.at[c], right(i, g, c), right_sem.at[c]).start()
+
+    def arrive(d, c):
+        for way in range(2):
+            @pl.when(has(way, d))
+            def _():
+                s = origin(way, d)
+                here = right(i, s, c)
+                hop(here, s, d - 1, c, way).wait_recv()
+                if d < nreg - 1:
+                    @pl.when(onward(way, d))
+                    def _():
+                        hop(here, s, d, c, way).start()
+                spread(here, s, c)
+
+    def pass_on(s, c):
+        for k in range(1, nx):
+            here = right((x - k + nx) % nx * 2 + core, s, c)
+            remote(here, here, x_send.at[k - 1, s, c], x_recv.at[k - 1, s, c], x_at(k)).wait_recv()
+            remote(here, here, fwd_send.at[k - 1, s, c], fwd_recv.at[k - 1, s, c], {"row": sib}).start()
+
+    def cross(d, c):
+        if d == 0:
+            pass_on(g, c)
+            return
+        for way in range(2):
+            @pl.when(has(way, d))
+            def _():
+                pass_on(origin(way, d), c)
+
+    ahead = min(2, chunks)
+    for c in range(ahead):
+        send_partials(c)
+    for tick in range(chunks + nreg):
+        if tick < chunks:
+            finish(tick)
+            if tick + ahead < chunks:
+                send_partials(tick + ahead)
+        for d in range(1, nreg):
+            if 0 <= tick - d < chunks:
+                arrive(d, tick - d)
+        for d in range(nreg):
+            if 0 <= tick - d - 1 < chunks:
+                cross(d, tick - d - 1)
 
     for c in range(chunks):
-        for q in range(1, nreg):
-            here = right(i, region_at(q), c)
-            remote(here, here, reg_send.at[q - 1, c], reg_recv.at[q - 1, c], reg_at(q)).wait_recv()
-            kept.append(spread(here, region_at(q), q, c))
-
-    for c in range(chunks):
-        for q in range(nreg):
+        pltpu.make_async_copy(stage.at[c], right(i, g, c), right_sem.at[c]).wait()
+        for s in range(nreg):
+            here = right(i, s, c)
+            for k in range(1, ncol):
+                there = left((j - k + ncol) % ncol, s, c)
+                copy = remote(there, there, col_send.at[k - 1, s, c], col_recv.at[k - 1, s, c], col_at(k))
+                copy.wait_recv()
+                copy.wait_send()
+            there = right(sib, s, c)
+            copy = remote(there, there, sib_send.at[s, c], sib_recv.at[s, c], {"row": sib})
+            copy.wait_recv()
+            copy.wait_send()
             for k in range(1, nx):
-                here = right((x - k + nx) % nx * 2 + core, region_at(q), c)
-                remote(here, here, x_send.at[k - 1, q, c], x_recv.at[k - 1, q, c], x_at(k)).wait_recv()
-                start(
-                    here, here, fwd_send.at[k - 1, q, c], fwd_recv.at[k - 1, q, c], {"row": sib}
-                )
-
-    for c in range(chunks):
-        for q in range(nreg):
-            region = region_at(q)
-            for k in range(1, ncol):
-                here = left((j - k + ncol) % ncol, region, c)
-                remote(here, here, col_send.at[k - 1, q, c], col_recv.at[k - 1, q, c], col_at(k)).wait_recv()
-            here = right(sib, region, c)
-            remote(here, here, sib_send.at[q, c], sib_recv.at[q, c], {"row": sib}).wait_recv()
-            for k in range(1, nx):
-                here = right((x - k + nx) % nx * 2 + 1 - core, region, c)
-                remote(here, here, fwd_send.at[k - 1, q, c], fwd_recv.at[k - 1, q, c], {"row": sib}).wait_recv()
+                there = right((x - k + nx) % nx * 2 + 1 - core, s, c)
+                copy = remote(there, there, fwd_send.at[k - 1, s, c], fwd_recv.at[k - 1, s, c], {"row": sib})
+                copy.wait_recv()
+                copy.wait_send()
+                remote(here, here, x_send.at[k - 1, s, c], x_recv.at[k - 1, s, c], x_at(k)).wait_send()
+            pltpu.make_async_copy(here, left(j, s, c), left_sem.at[s, c]).wait()
+        for way in range(2):
+            for d in range(nreg - 1):
+                @pl.when(onward(way, d))
+                def _():
+                    s = origin(way, d)
+                    hop(right(i, s, c), s, d, c, way).wait_send()
     for copy in sent:
         copy.wait_send()
-    for copy in kept:
-        copy.wait()
 
 
 def gathered_panels(shape, activity, basis, region_of):
@@ -285,7 +335,8 @@
             pltpu.VMEM((nreg - 1, chunks, width, span), jnp.bfloat16),
             pltpu.VMEM((chunks, width, span), jnp.bfloat16),
         ]
-        + [dma((nreg - 1, chunks))] * 4
+        + [dma((nreg - 1, chunks))] * 2
+        + [dma((2, nreg - 1, chunks))] * 2
         + [dma((ncol - 1, nreg, chunks))] * 2
         + [dma((nx - 1, nreg, chunks))] * 2
         + [dma((nreg, chunks))] * 2

time: 91.4 us -> 83.2 us (0.910)
  the two profiles are of different devices: /device:TPU:25 before, /device:TPU:0 now
where the time goes in v4:
time: 83.2 us; the launch traced here: 82.9 us
  Pallas kernels  76.6 us (92%)
  local copies, waits for them, and re-layouts  6.3 us (8%)
    pallas_call x1, Pallas kernels, gathered_panels(): pl.pallas_call(functools.partial(panels_kernel, shape, chunks), in_specs=...  52.9 us
    pallas_call x1, Pallas kernels, covariances(): pl.pallas_call(functools.partial(pair_kernel, nlag, group), grid_spec=plt...  23.7 us
    unnamed x10, local copies, waits for them, and re-layouts  6.3 us

profile of v4, /device:TPU:0, one launch (start us, length us, event | category | flops | bytes accessed | tf_op | source)
XLA Modules:
  0.0 82.9 jit_solution(2174816887844456481)
XLA Ops:
  0.0 0.0 copy-start.2
  0.0 0.8 copy.7.pairs_ref
  0.8 1.1 %copy.6.basis_ref = bf16[768,64]{1,0:T(8,128)(2,1)S(1)} copy(bf16[768,64]{0,1:T(8,128)(2,1)} %param.6) | data formatting | bytes 196608 | tf_op args[1]
  1.8 0.0 copy-start.1
  1.8 1.9 %copy-done.1 = bf16[768,2048]{1,0:T(8,128)(2,1)S(1)} copy-done((bf16[768,2048]{1,0:T(8,128)(2,1)S(1)}, bf16[768,2048]{1,0:T(8,128)(2,1)}, u32[]{:S(2)}) %copy-start.1) | copy-done | bytes 3145752
  3.7 0.0 copy-start.3
  3.7 0.7 copy-done.3
  4.4 52.9 %shard_map.55 = (bf16[8,64,2048]{2,1,0:T(8,128)(2,1)S(1)}, bf16[16,64,2048]{2,1,0:T(8,128)(2,1)S(1)}) custom-call(s32[6]{0:T(128)S(1)} %copy-done.3, bf16[768,64]{1,0:T(8,128)(2,1)S(1)} %copy.6.basis_ref, bf16[768,2048]{1,0:T(8,128)(2,1)S(1)} %copy-done.1), custom_call_target="tpu_custom_call" | custom-call | tf_op jit(solution)/shard_map/pallas_call | solution.py:320
  57.3 0.0 copy-start
  57.4 1.9 %copy-done = bf16[16,64,2048]{2,1,0:T(8,128)(2,1)} copy-done((bf16[16,64,2048]{2,1,0:T(8,128)(2,1)}, bf16[16,64,2048]{2,1,0:T(8,128)(2,1)S(1)}, u32[]{:S(2)}) %copy-start) | copy-done | bytes 4194328
  59.3 0.0 copy-done.2
  59.3 23.7 %shard_map.56 = bf16[32,64,512]{2,1,0:T(8,128)(2,1)} custom-call(s32[32,2]{1,0:T(8,128)S(1)} %copy.7.pairs_ref, s32[8]{0:T(128)S(1)} %copy-done.2, bf16[8,64,2048]{2,1,0:T(8,128)(2,1)S(1)} %get-tuple-element.7.lefts_ref, bf16[16,64,2048]{2,1,0:T(8,128)(2,1)} %copy-done), custom_call_target="tpu_custom_call" | custom-call | tf_op jit(solution)/shard_map/pallas_call | solution.py:86
Async XLA Ops:
  0.0 59.3 %copy-start.2 = (s32[8]{0:T(128)S(1)}, s32[8]{0:T(128)}, u32[]{:S(2)}) copy-start(s32[8]{0:T(128)} %lags_ref.1) | copy-start | bytes 100
  1.8 1.9 %copy-start.1 = (bf16[768,2048]{1,0:T(8,128)(2,1)S(1)}, bf16[768,2048]{1,0:T(8,128)(2,1)}, u32[]{:S(2)}) copy-start(bf16[768,2048]{1,0:T(8,128)(2,1)} %act_ref.1) | copy-start | bytes 9437188
  3.7 0.7 copy-start.3
  57.3 1.9 %copy-start = (bf16[16,64,2048]{2,1,0:T(8,128)(2,1)}, bf16[16,64,2048]{2,1,0:T(8,128)(2,1)S(1)}, u32[]{:S(2)}) copy-start(bf16[16,64,2048]{2,1,0:T(8,128)(2,1)S(1)} %get-tuple-element.8.rights_ref) | copy-start | bytes 12582916

commit v5 on v4

--- a/solution.py
+++ b/solution.py
@@ -9,6 +9,7 @@
 
 BLK = 128
 CHUNKS = 4
+SPLIT = 4
 
 
 def shifted(x, s):
@@ -24,21 +25,21 @@
 
 
 def left_stack(left):
-    return [left, shifted(left, -1)]
+    return [left] + [shifted(left, -s) for s in range(1, SPLIT)]
 
 
 def right_stack(right, nlag):
-    return [right] + [shifted(right, s) for s in range(2, nlag, 2)]
+    return [right] + [shifted(right, s) for s in range(SPLIT, nlag, SPLIT)]
 
 
 def one_pair(nlag, lags_ref, lhs, rhs, prod):
-    width, bins = lhs.shape[0] // 2, lhs.shape[1]
+    width, bins = lhs.shape[0] // SPLIT, lhs.shape[1]
     acc = lax.dot_general(
         lhs, rhs, (((1,), (1,)), ((), ())), preferred_element_type=jnp.float32
     )
     acc = acc * (1.0 / bins**0.5)
     for lag in range(nlag):
-        m1, m2 = lag % 2, lag // 2
+        m1, m2 = lag % SPLIT, lag // SPLIT
         prod[lag] = acc[m1 * width:(m1 + 1) * width, m2 * width:(m2 + 1) * width]
     return jnp.concatenate([prod[lags_ref[m]] for m in range(nlag)], axis=1).astype(jnp.bfloat16)
 
@@ -77,12 +78,12 @@
     nlag = lags.shape[0]
     _, width, bins = lefts.shape
     out_shape = jax.ShapeDtypeStruct((npairs, width, nlag * width), jnp.bfloat16)
-    panels = 3 * lefts.shape[0] + 5 * rights.shape[0]
+    panels = (1 + SPLIT) * lefts.shape[0] + (1 + nlag // SPLIT) * rights.shape[0]
     params = pltpu.CompilerParams(
         dimension_semantics=("arbitrary",), vmem_limit_bytes=48 << 20
     )
     if panels * width * bins * 2 <= 36 << 20:
-        group = 4
+        group = 8
         return pl.pallas_call(
             functools.partial(pair_kernel, nlag, group),
             grid_spec=pltpu.PrefetchScalarGridSpec(
@@ -93,8 +94,8 @@
                     (group, width, nlag * width), lambda p, pairs, lags: (p, 0, 0)
                 ),
                 scratch_shapes=[
-                    pltpu.VMEM((lefts.shape[0], 2 * width, bins), jnp.bfloat16),
-                    pltpu.VMEM((rights.shape[0], nlag // 2 * width, bins), jnp.bfloat16),
+                    pltpu.VMEM((lefts.shape[0], SPLIT * width, bins), jnp.bfloat16),
+                    pltpu.VMEM((rights.shape[0], nlag // SPLIT * width, bins), jnp.bfloat16),
                     pltpu.VMEM((group, nlag, width, width), jnp.float32),
                 ],
             ),

time: 83.2 us -> 78.5 us (0.944)
  Pallas kernels: 76.6 us -> 71.9 us
    pallas_call x1, Pallas kernels: 23.7 us -> 19 us  [covariances(): pl.pallas_call(functools.partial(pair_kernel, nlag, group), grid_spec=plt...]
where the time goes in v5:
time: 78.5 us; the launch traced here: 78.2 us
  Pallas kernels  71.9 us (92%)
  local copies, waits for them, and re-layouts  6.3 us (8%)
    pallas_call x1, Pallas kernels, gathered_panels(): pl.pallas_call(functools.partial(panels_kernel, shape, chunks), in_specs=...  52.9 us
    pallas_call x1, Pallas kernels, covariances(): pl.pallas_call(functools.partial(pair_kernel, nlag, group), grid_spec=plt...  19 us
    unnamed x10, local copies, waits for them, and re-layouts  6.3 us

profile of v5, /device:TPU:0, one launch (start us, length us, event | category | flops | bytes accessed | tf_op | source)
XLA Modules:
  0.0 78.2 jit_solution(14821762882492058224)
XLA Ops:
  0.0 0.0 copy-start.2
  0.0 0.8 copy.7.pairs_ref
  0.8 1.1 %copy.6.basis_ref = bf16[768,64]{1,0:T(8,128)(2,1)S(1)} copy(bf16[768,64]{0,1:T(8,128)(2,1)} %param.6) | data formatting | bytes 196608 | tf_op args[1]
  1.8 0.0 copy-start.1
  1.8 1.9 %copy-done.1 = bf16[768,2048]{1,0:T(8,128)(2,1)S(1)} copy-done((bf16[768,2048]{1,0:T(8,128)(2,1)S(1)}, bf16[768,2048]{1,0:T(8,128)(2,1)}, u32[]{:S(2)}) %copy-start.1) | copy-done | bytes 3145752
  3.7 0.0 copy-start.3
  3.7 0.7 copy-done.3
  4.4 52.9 %shard_map.55 = (bf16[8,64,2048]{2,1,0:T(8,128)(2,1)S(1)}, bf16[16,64,2048]{2,1,0:T(8,128)(2,1)S(1)}) custom-call(s32[6]{0:T(128)S(1)} %copy-done.3, bf16[768,64]{1,0:T(8,128)(2,1)S(1)} %copy.6.basis_ref, bf16[768,2048]{1,0:T(8,128)(2,1)S(1)} %copy-done.1), custom_call_target="tpu_custom_call" | custom-call | tf_op jit(solution)/shard_map/pallas_call | solution.py:321
  57.3 0.0 copy-start
  57.4 1.9 %copy-done = bf16[16,64,2048]{2,1,0:T(8,128)(2,1)} copy-done((bf16[16,64,2048]{2,1,0:T(8,128)(2,1)}, bf16[16,64,2048]{2,1,0:T(8,128)(2,1)S(1)}, u32[]{:S(2)}) %copy-start) | copy-done | bytes 4194328
  59.3 0.0 copy-done.2
  59.3 19.0 %shard_map.56 = bf16[32,64,512]{2,1,0:T(8,128)(2,1)} custom-call(s32[32,2]{1,0:T(8,128)S(1)} %copy.7.pairs_ref, s32[8]{0:T(128)S(1)} %copy-done.2, bf16[8,64,2048]{2,1,0:T(8,128)(2,1)S(1)} %get-tuple-element.7.lefts_ref, bf16[16,64,2048]{2,1,0:T(8,128)(2,1)} %copy-done), custom_call_target="tpu_custom_call" | custom-call | tf_op jit(solution)/shard_map/pallas_call | solution.py:87
Async XLA Ops:
  0.0 59.3 %copy-start.2 = (s32[8]{0:T(128)S(1)}, s32[8]{0:T(128)}, u32[]{:S(2)}) copy-start(s32[8]{0:T(128)} %lags_ref.1) | copy-start | bytes 100
  1.8 1.9 %copy-start.1 = (bf16[768,2048]{1,0:T(8,128)(2,1)S(1)}, bf16[768,2048]{1,0:T(8,128)(2,1)}, u32[]{:S(2)}) copy-start(bf16[768,2048]{1,0:T(8,128)(2,1)} %act_ref.1) | copy-start | bytes 9437188
  3.7 0.7 copy-start.3
  57.3 1.9 %copy-start = (bf16[16,64,2048]{2,1,0:T(8,128)(2,1)}, bf16[16,64,2048]{2,1,0:T(8,128)(2,1)S(1)}, u32[]{:S(2)}) copy-start(bf16[16,64,2048]{2,1,0:T(8,128)(2,1)S(1)} %get-tuple-element.8.rights_ref) | copy-start | bytes 12582916

commit v6 on v5

--- a/solution.py
+++ b/solution.py
@@ -44,21 +44,42 @@
     return jnp.concatenate([prod[lags_ref[m]] for m in range(nlag)], axis=1).astype(jnp.bfloat16)
 
 
-def pair_kernel(nlag, group, pairs_ref, lags_ref, lefts_ref, rights_ref, out_ref, lhs, rhs, prod):
+def pair_kernel(
+    nlag, group, pairs_ref, lags_ref, lefts_ref, rights_ref, out_ref, lhs, rhs, prod,
+    left_sem, right_sem,
+):
     width = lefts_ref.shape[1]
     step = pl.program_id(0)
 
     @pl.when(step == 0)
     def _():
+        def load_left(r):
+            return pltpu.make_async_copy(lefts_ref.at[r], lhs.at[r, :width, :], left_sem.at[r])
+
+        def load_right(r):
+            return pltpu.make_async_copy(rights_ref.at[r], rhs.at[r, :width, :], right_sem.at[r])
+
         @pl.loop(0, lefts_ref.shape[0])
         def _(r):
-            for m, x in enumerate(left_stack(lefts_ref[r])):
-                lhs[r, m * width:(m + 1) * width, :] = x
+            load_left(r).start()
 
         @pl.loop(0, rights_ref.shape[0])
         def _(r):
-            for m, x in enumerate(right_stack(rights_ref[r], nlag)):
-                rhs[r, m * width:(m + 1) * width, :] = x
+            load_right(r).start()
+
+        @pl.loop(0, lefts_ref.shape[0])
+        def _(r):
+            load_left(r).wait()
+            stack = left_stack(lhs[r, :width, :])
+            for m in range(1, len(stack)):
+                lhs[r, m * width:(m + 1) * width, :] = stack[m]
+
+        @pl.loop(0, rights_ref.shape[0])
+        def _(r):
+            load_right(r).wait()
+            stack = right_stack(rhs[r, :width, :], nlag)
+            for m in range(1, len(stack)):
+                rhs[r, m * width:(m + 1) * width, :] = stack[m]
 
     for q in range(group):
         p = step * group + q
@@ -89,7 +110,7 @@
             grid_spec=pltpu.PrefetchScalarGridSpec(
                 num_scalar_prefetch=2,
                 grid=(npairs // group,),
-                in_specs=[pl.BlockSpec(memory_space=pltpu.VMEM)] * 2,
+                in_specs=[pl.BlockSpec(memory_space=pltpu.HBM)] * 2,
                 out_specs=pl.BlockSpec(
                     (group, width, nlag * width), lambda p, pairs, lags: (p, 0, 0)
                 ),
@@ -97,6 +118,8 @@
                     pltpu.VMEM((lefts.shape[0], SPLIT * width, bins), jnp.bfloat16),
                     pltpu.VMEM((rights.shape[0], nlag // SPLIT * width, bins), jnp.bfloat16),
                     pltpu.VMEM((group, nlag, width, width), jnp.float32),
+                    pltpu.SemaphoreType.DMA((lefts.shape[0],)),
+                    pltpu.SemaphoreType.DMA((rights.shape[0],)),
                 ],
             ),
             out_shape=out_shape,
@@ -121,7 +144,7 @@
 
 def panels_kernel(
     shape, chunks, region_ref, basis_ref, act_ref, lefts_ref, rights_ref,
-    own, send, landed, stage,
+    act, act_sem, own, send, landed, stage,
     rs_send, rs_recv, reg_send, reg_recv, col_send, col_recv,
     x_send, x_recv, sib_send, sib_recv, fwd_send, fwd_recv, left_sem, right_sem,
 ):
@@ -147,6 +170,14 @@
     peers += [col_at(k) for k in range(1, ncol)]
     peers += [x_at(k) for k in range(1, nx)]
     peers += [{"row": sib}]
+    loads = [
+        pltpu.make_async_copy(
+            act_ref.at[:, pl.ds(c * span, span)], act.at[c], act_sem.at[c]
+        )
+        for c in range(chunks)
+    ]
+    for load in loads:
+        load.start()
     barrier = pltpu.get_barrier_semaphore()
     for peer in peers:
         pl.semaphore_signal(
@@ -182,8 +213,9 @@
     masked = jnp.concatenate(pieces, axis=0)
 
     def send_partials(c):
+        loads[c].wait()
         part = lax.dot_general(
-            masked, act_ref[:, c * span:(c + 1) * span], (((0,), (0,)), ((), ())),
+            masked, act[c], (((0,), (0,)), ((), ())),
             preferred_element_type=jnp.float32,
         )
         own[c] = part
@@ -323,7 +355,7 @@
         in_specs=[
             pl.BlockSpec(memory_space=pltpu.SMEM),
             pl.BlockSpec(memory_space=pltpu.VMEM),
-            pl.BlockSpec(memory_space=pltpu.VMEM),
+            pl.BlockSpec(memory_space=pltpu.HBM),
         ],
         out_specs=[pl.BlockSpec(memory_space=pl.ANY)] * 2,
         out_shape=[
@@ -331,6 +363,8 @@
             jax.ShapeDtypeStruct((nrow * nreg, width, bins), jnp.bfloat16),
         ],
         scratch_shapes=[
+            pltpu.VMEM((chunks, activity.shape[0], span), jnp.bfloat16),
+            dma((chunks,)),
             pltpu.VMEM((chunks, nreg * width, span), jnp.float32),
             pltpu.VMEM((chunks, nreg * width, span), jnp.bfloat16),
             pltpu.VMEM((nreg - 1, chunks, width, span), jnp.bfloat16),

time: 78.5 us -> 77 us (0.981)
  Pallas kernels: 71.9 us -> 70.5 us
    pallas_call x1, Pallas kernels: 19 us -> 17.1 us  [covariances(): pl.pallas_call(functools.partial(pair_kernel, nlag, group), grid_spec=plt...]
where the time goes in v6:
time: 77 us; the launch traced here: 76.8 us
  Pallas kernels  70.5 us (92%)
  local copies, waits for them, and re-layouts  6.3 us (8%)
    pallas_call x1, Pallas kernels, gathered_panels(): pl.pallas_call(functools.partial(panels_kernel, shape, chunks), in_specs=...  53.4 us
    pallas_call x1, Pallas kernels, covariances(): pl.pallas_call(functools.partial(pair_kernel, nlag, group), grid_spec=plt...  17.1 us
    unnamed x10, local copies, waits for them, and re-layouts  6.3 us

profile of v6, /device:TPU:0, one launch (start us, length us, event | category | flops | bytes accessed | tf_op | source)
XLA Modules:
  0.0 76.8 jit_solution(7245018099836568446)
XLA Ops:
  0.0 0.0 copy-start.2
  0.0 0.8 %copy.7.pairs_ref = s32[32,2]{1,0:T(8,128)S(1)} copy(s32[32,2]{0,1:T(2,128)} %param.8) | data formatting | bytes 512 | tf_op args[3]
  0.8 1.1 %copy.6.basis_ref = bf16[768,64]{1,0:T(8,128)(2,1)S(1)} copy(bf16[768,64]{0,1:T(8,128)(2,1)} %param.6) | data formatting | bytes 196608 | tf_op args[1]
  1.8 0.0 copy-start.1
  1.8 1.9 %copy-done.1 = bf16[768,2048]{1,0:T(8,128)(2,1)S(1)} copy-done((bf16[768,2048]{1,0:T(8,128)(2,1)S(1)}, bf16[768,2048]{1,0:T(8,128)(2,1)}, u32[]{:S(2)}) %copy-start.1) | copy-done | bytes 3145752
  3.7 0.0 copy-start.3
  3.7 0.7 copy-done.3
  4.4 53.4 %shard_map.55 = (bf16[8,64,2048]{2,1,0:T(8,128)(2,1)S(1)}, bf16[16,64,2048]{2,1,0:T(8,128)(2,1)S(1)}) custom-call(s32[6]{0:T(128)S(1)} %copy-done.3, bf16[768,64]{1,0:T(8,128)(2,1)S(1)} %copy.6.basis_ref, bf16[768,2048]{1,0:T(8,128)(2,1)S(1)} %copy-done.1), custom_call_target="tpu_custom_call" | custom-call | tf_op jit(solution)/shard_map/pallas_call | solution.py:353
  57.8 0.0 copy-start
  57.8 1.9 %copy-done = bf16[16,64,2048]{2,1,0:T(8,128)(2,1)} copy-done((bf16[16,64,2048]{2,1,0:T(8,128)(2,1)}, bf16[16,64,2048]{2,1,0:T(8,128)(2,1)S(1)}, u32[]{:S(2)}) %copy-start) | copy-done | bytes 4194328
  59.7 0.0 copy-done.2
  59.7 17.1 %shard_map.56 = bf16[32,64,512]{2,1,0:T(8,128)(2,1)} custom-call(s32[32,2]{1,0:T(8,128)S(1)} %copy.7.pairs_ref, s32[8]{0:T(128)S(1)} %copy-done.2, bf16[8,64,2048]{2,1,0:T(8,128)(2,1)S(1)} %get-tuple-element.7.lefts_ref, bf16[16,64,2048]{2,1,0:T(8,128)(2,1)} %copy-done), custom_call_target="tpu_custom_call" | custom-call | tf_op jit(solution)/shard_map/pallas_call | solution.py:108
Async XLA Ops:
  0.0 59.7 %copy-start.2 = (s32[8]{0:T(128)S(1)}, s32[8]{0:T(128)}, u32[]{:S(2)}) copy-start(s32[8]{0:T(128)} %lags_ref.1) | copy-start | bytes 100
  1.8 1.9 %copy-start.1 = (bf16[768,2048]{1,0:T(8,128)(2,1)S(1)}, bf16[768,2048]{1,0:T(8,128)(2,1)}, u32[]{:S(2)}) copy-start(bf16[768,2048]{1,0:T(8,128)(2,1)} %act_ref.1) | copy-start | bytes 9437188
  3.7 0.7 copy-start.3
  57.8 1.9 %copy-start = (bf16[16,64,2048]{2,1,0:T(8,128)(2,1)}, bf16[16,64,2048]{2,1,0:T(8,128)(2,1)S(1)}, u32[]{:S(2)}) copy-start(bf16[16,64,2048]{2,1,0:T(8,128)(2,1)S(1)} %get-tuple-element.8.rights_ref) | copy-start | bytes 12582916

commit v7 on v6

--- a/solution.py
+++ b/solution.py
@@ -101,7 +101,7 @@
     out_shape = jax.ShapeDtypeStruct((npairs, width, nlag * width), jnp.bfloat16)
     panels = (1 + SPLIT) * lefts.shape[0] + (1 + nlag // SPLIT) * rights.shape[0]
     params = pltpu.CompilerParams(
-        dimension_semantics=("arbitrary",), vmem_limit_bytes=48 << 20
+        dimension_semantics=("arbitrary",), vmem_limit_bytes=62 << 20
     )
     if panels * width * bins * 2 <= 36 << 20:
         group = 8
@@ -378,7 +378,7 @@
         + [dma((nx - 1, nreg, chunks))] * 2
         + [dma((nreg, chunks)), dma((chunks,))],
         compiler_params=pltpu.CompilerParams(
-            collective_id=0, has_side_effects=True, vmem_limit_bytes=40 << 20
+            collective_id=0, has_side_effects=True, vmem_limit_bytes=62 << 20
         ),
     )(region_of, basis, activity)
 

time: 77 us -> 76.6 us (level)
  local copies, waits for them, and re-layouts: 6.3 us -> 3.06 us
  Pallas kernels: 70.5 us -> 73.3 us
    unnamed x10 -> x2, local copies, waits for them, and re-layouts: 6.3 us -> 3.06 us
    pallas_call x1, Pallas kernels: 53.4 us -> 55.5 us  [gathered_panels(): pl.pallas_call(functools.partial(panels_kernel, shape, chunks), in_specs=...]
where the time goes in v7:
time: 76.6 us; the launch traced here: 76.3 us
  Pallas kernels  73.3 us (96%)
  local copies, waits for them, and re-layouts  3.06 us (4%)
    pallas_call x1, Pallas kernels, gathered_panels(): pl.pallas_call(functools.partial(panels_kernel, shape, chunks), in_specs=...  55.5 us
    pallas_call x1, Pallas kernels, covariances(): pl.pallas_call(functools.partial(pair_kernel, nlag, group), grid_spec=plt...  17.8 us
    unnamed x2, local copies, waits for them, and re-layouts  3.06 us

profile of v7, /device:TPU:0, one launch (start us, length us, event | category | flops | bytes accessed | tf_op | source)
XLA Modules:
  0.0 76.3 jit_solution(8607283032756307138)
XLA Ops:
  0.0 1.4 %copy.7.pairs_ref = s32[32,2]{1,0:T(8,128)} copy(s32[32,2]{0,1:T(2,128)} %param.8) | data formatting | bytes 512 | tf_op args[3]
  1.4 1.7 %copy.6.basis_ref = bf16[768,64]{1,0:T(8,128)(2,1)} copy(bf16[768,64]{0,1:T(8,128)(2,1)} %param.6) | data formatting | bytes 196608 | tf_op args[1]
  3.1 55.5 %shard_map.55 = (bf16[8,64,2048]{2,1,0:T(8,128)(2,1)}, bf16[16,64,2048]{2,1,0:T(8,128)(2,1)}) custom-call(s32[6]{0:T(128)} %region_ref.1, bf16[768,64]{1,0:T(8,128)(2,1)} %copy.6.basis_ref, bf16[768,2048]{1,0:T(8,128)(2,1)} %act_ref.1), custom_call_target="tpu_custom_call" | custom-call | tf_op jit(solution)/shard_map/pallas_call | solution.py:353
  58.5 17.8 %shard_map.56 = bf16[32,64,512]{2,1,0:T(8,128)(2,1)} custom-call(s32[32,2]{1,0:T(8,128)} %copy.7.pairs_ref, s32[8]{0:T(128)} %lags_ref.1, bf16[8,64,2048]{2,1,0:T(8,128)(2,1)} %get-tuple-element.7.lefts_ref, bf16[16,64,2048]{2,1,0:T(8,128)(2,1)} %get-tuple-element.8.rights_ref), custom_call_target="tpu_custom_call" | custom-call | tf_op jit(solution)/shard_map/pallas_call | solution.py:108

commit v8 on v7

--- a/solution.py
+++ b/solution.py
@@ -8,7 +8,7 @@
 from jax.sharding import PartitionSpec as P
 
 BLK = 128
-CHUNKS = 4
+CHUNKS = 8
 SPLIT = 4
 
 
@@ -298,7 +298,7 @@
             def _():
                 pass_on(origin(way, d), c)
 
-    ahead = min(2, chunks)
+    ahead = min(4, chunks)
     for c in range(ahead):
         send_partials(c)
     for tick in range(chunks + nreg):

time: 76.6 us -> 82 us (1.070)
  Pallas kernels: 73.3 us -> 78.7 us
    pallas_call x1, Pallas kernels: 55.5 us -> 60.8 us  [gathered_panels(): pl.pallas_call(functools.partial(panels_kernel, shape, chunks), in_specs=...]
where the time goes in v8:
time: 82 us; the launch traced here: 81.7 us
  Pallas kernels  78.7 us (96%)
  local copies, waits for them, and re-layouts  3.06 us (4%)
    pallas_call x1, Pallas kernels, gathered_panels(): pl.pallas_call(functools.partial(panels_kernel, shape, chunks), in_specs=...  60.8 us
    pallas_call x1, Pallas kernels, covariances(): pl.pallas_call(functools.partial(pair_kernel, nlag, group), grid_spec=plt...  17.8 us
    unnamed x2, local copies, waits for them, and re-layouts  3.06 us

profile of v8, /device:TPU:0, one launch (start us, length us, event | category | flops | bytes accessed | tf_op | source)
XLA Modules:
  0.0 81.7 jit_solution(8731582445309583229)
XLA Ops:
  0.0 1.4 %copy.7.pairs_ref = s32[32,2]{1,0:T(8,128)} copy(s32[32,2]{0,1:T(2,128)} %param.8) | data formatting | bytes 512 | tf_op args[3]
  1.4 1.7 %copy.6.basis_ref = bf16[768,64]{1,0:T(8,128)(2,1)} copy(bf16[768,64]{0,1:T(8,128)(2,1)} %param.6) | data formatting | bytes 196608 | tf_op args[1]
  3.1 60.8 %shard_map.55 = (bf16[8,64,2048]{2,1,0:T(8,128)(2,1)}, bf16[16,64,2048]{2,1,0:T(8,128)(2,1)}) custom-call(s32[6]{0:T(128)} %region_ref.1, bf16[768,64]{1,0:T(8,128)(2,1)} %copy.6.basis_ref, bf16[768,2048]{1,0:T(8,128)(2,1)} %act_ref.1), custom_call_target="tpu_custom_call" | custom-call | tf_op jit(solution)/shard_map/pallas_call | solution.py:353
  63.9 17.8 %shard_map.56 = bf16[32,64,512]{2,1,0:T(8,128)(2,1)} custom-call(s32[32,2]{1,0:T(8,128)} %copy.7.pairs_ref, s32[8]{0:T(128)} %lags_ref.1, bf16[8,64,2048]{2,1,0:T(8,128)(2,1)} %get-tuple-element.7.lefts_ref, bf16[16,64,2048]{2,1,0:T(8,128)(2,1)} %get-tuple-element.8.rights_ref), custom_call_target="tpu_custom_call" | custom-call | tf_op jit(solution)/shard_map/pallas_call | solution.py:108
